TPU v7x, 256 devices: a whole 4x4x8 slice. The times are simulated.
256 devices in a mesh: shard: 32 (over z, y), dp: 8 (over x, core).
Axes of the slice: x: 4, y: 4, z: 8, core: 2. Of those that a mesh axis runs over, the one named last changes fastest.
Arguments:
- cold_table: bfloat16 [65536, 256], P('shard'), may hold values from -6 to 6
- cold_accum: float32 [65536], P('shard'), may hold values from 0.005 to 0.5
- dither_bits: int32 [65536, 256], P('shard'), may hold values from 0 to 65280
- hot_table: float32 [1024, 256], replicated, may hold values from -6 to 6
- hot_accum: float32 [1024], replicated, may hold values from 1 to 100
- w_flat: bfloat16 [4096, 512], replicated, may hold values from -0.09375 to 0.09375
- w_inter: bfloat16 [256, 512], replicated, may hold values from -0.09375 to 0.09375
- hidden_bias: float32 [512], replicated, may hold values from -1 to 1
- w_out: float32 [512], replicated, may hold values from -0.25 to 0.25
- targets: float32 [131072], P(('shard', 'dp')), may hold values from 0 to 1
- hot_ids: int32 [131072, 8], P(('shard', 'dp')), may hold values from 0 to 1023
- cold_slots: int32 [131072, 8], P(('shard', 'dp')), may hold values from 0 to 2047, as said below
- requests: int32 [16384, 64], P(('shard', 'dp')), may hold values from 0 to 2047, as said below
- counts: int32 [512, 32], P(('shard', 'dp')), may hold values from 1 to 64, as said below
Outputs:
- cold_out: bfloat16 [65536, 256], P('shard')
- cold_accum_out: float32 [65536], P('shard')
- hot_out: float32 [1024, 256], replicated
- hot_accum_out: float32 [1024], replicated
Inputs may be any that keep to these rules, and one draw needn't show every extreme that they name: `requests`: in each row of 64 entries (one device, micro-batch and shard) the entries name distinct rows of that shard's 2048; only the first counts-many are live, the rest name arbitrary rows. `counts`: in every draw, each device has in each micro-batch a shard with exactly 64 live slots. `cold_slots`: index into its device's request rows of that micro-batch, shard * 64 + slot; always a live slot, and every live slot is named by some lookup.
All inputs are finite; a program needn't handle non-finite values.
Results may differ from a plain program's by a relative error of at most 0.001.
The roundings to bfloat16 on the way count: a program that leaves them out, or rounds other values in their place, can miss the bound.
Values may be sent and summed in bfloat16 or wider, within the bound.
No kernel may reach another device: no remote copies, remote signals or barrier semaphores. Data moves between devices by JAX's collectives and lax.ppermute only.
A program may use at most 128 MiB of HBM per device.

v0:
```python
import jax
import jax.numpy as jnp
from jax import lax
from jax.sharding import PartitionSpec as P

MB = 2
BATCH = 256
learn_rate = 0.3


def backprop(stacked, targets, w_flat, w_inter, hidden_bias, w_out):
    row_count, feature_count, row_width = stacked.shape
    flattened = stacked.reshape(row_count, feature_count * row_width)
    pair_dots = (
        jnp.einsum("sfe,sge->sfg", stacked, stacked, preferred_element_type=jnp.float32)
        * row_width ** (-0.5)
    ).astype(jnp.bfloat16)
    pre_act = jnp.dot(flattened, w_flat, preferred_element_type=jnp.float32)
    pre_act = pre_act + jnp.dot(
        pair_dots.reshape(row_count, feature_count * feature_count),
        w_inter,
        preferred_element_type=jnp.float32,
    )
    pre_act = pre_act + hidden_bias
    gated = jax.nn.sigmoid(pre_act)
    logits = jnp.sum(pre_act * gated * w_out, axis=-1)
    residual = jax.nn.sigmoid(logits) - targets
    slopes = (residual[:, None] * w_out * gated * (1.0 + pre_act * (1.0 - gated))).astype(
        jnp.bfloat16
    )
    back_flat = jnp.dot(slopes, w_flat.T, preferred_element_type=jnp.float32)
    back_pairs = jnp.dot(slopes, w_inter.T, preferred_element_type=jnp.float32).reshape(
        row_count, feature_count, feature_count
    )
    mirror = ((back_pairs + jnp.swapaxes(back_pairs, 1, 2)) * row_width ** (-0.5)).astype(
        jnp.bfloat16
    )
    return back_flat.reshape(row_count, feature_count, row_width) + jnp.einsum(
        "sfg,sge->sfe", mirror, stacked, preferred_element_type=jnp.float32
    )


def adagrad_rows(table_rows, accum, gradient):
    accum_new = accum + jnp.mean(gradient * gradient, axis=-1)
    updated = table_rows - learn_rate * gradient / jnp.sqrt(accum_new)[:, None]
    return (updated, accum_new)


def requantize(updated, bits, touched):
    grid_step = jnp.max(jnp.abs(updated), axis=-1, keepdims=True) / 8.0
    dither = bits.astype(jnp.float32) * (1.0 / 65280.0) - 0.5
    return jnp.where(touched[:, None], updated + grid_step * dither, updated).astype(jnp.bfloat16)


def on_device(
    cold_table,
    cold_accum,
    dither_bits,
    hot_table,
    hot_accum,
    w_flat,
    w_inter,
    hidden_bias,
    w_out,
    targets,
    hot_ids,
    cold_slots,
    requests,
    counts,
):
    shards = lax.axis_size("shard")
    capacity = requests.shape[1]
    row_count = cold_table.shape[0]
    row_width = cold_table.shape[1]
    hot_count = hot_table.shape[0]
    cold_feats = cold_slots.shape[1]
    hot_grad = jnp.zeros((hot_count, row_width), jnp.float32)
    cold_grad = jnp.zeros((row_count, row_width), jnp.float32)
    touched = jnp.zeros((row_count,), jnp.float32)
    for micro_index in range(MB):
        asked_rows = requests[micro_index * shards : (micro_index + 1) * shards]
        requested = lax.all_to_all(asked_rows, "shard", split_axis=0, concat_axis=0, tiled=True)
        fetched_rows = lax.all_to_all(
            cold_table[requested], "shard", split_axis=0, concat_axis=0, tiled=True
        )
        first = micro_index * BATCH
        slot_part = cold_slots[first : first + BATCH]
        hot_part = hot_ids[first : first + BATCH]
        cold_vectors = fetched_rows.reshape(shards * capacity, row_width)[slot_part]
        stacked = jnp.concatenate([cold_vectors, hot_table[hot_part].astype(jnp.bfloat16)], axis=1)
        gradients = backprop(
            stacked, targets[first : first + BATCH], w_flat, w_inter, hidden_bias, w_out
        )
        slot_grad = jax.ops.segment_sum(
            gradients[:, :cold_feats].reshape(-1, row_width),
            slot_part.reshape(-1),
            num_segments=shards * capacity,
        )
        hot_term = jax.ops.segment_sum(
            gradients[:, cold_feats:].reshape(-1, row_width),
            hot_part.reshape(-1),
            num_segments=hot_count,
        )
        slot_grad, hot_term = (slot_grad.reshape(shards, capacity, row_width), hot_term)
        hot_grad = hot_grad + hot_term
        owner_grad, count_in = (
            lax.all_to_all(
                slot_grad.astype(jnp.bfloat16), "shard", split_axis=0, concat_axis=0, tiled=True
            ).astype(slot_grad.dtype),
            lax.all_to_all(counts[micro_index], "shard", split_axis=0, concat_axis=0, tiled=True),
        )
        cold_grad = cold_grad + jax.ops.segment_sum(
            owner_grad.reshape(-1, row_width), requested.reshape(-1), num_segments=row_count
        )
        live_mask = (jnp.arange(capacity, dtype=jnp.int32)[None, :] < count_in[:, None]).astype(
            jnp.float32
        )
        touched = touched + jax.ops.segment_sum(
            live_mask.reshape(-1), requested.reshape(-1), num_segments=row_count
        )
    summed_grad, summed_hits = (
        lax.psum(cold_grad.astype(jnp.bfloat16), "dp").astype(jnp.float32),
        lax.psum(touched.astype(jnp.bfloat16), "dp").astype(jnp.float32),
    )
    averaged = summed_grad / jnp.maximum(summed_hits, 1.0)[:, None]
    updated, cold_accum_out = adagrad_rows(cold_table.astype(jnp.float32), cold_accum, averaged)
    cold_out = requantize(updated, dither_bits, summed_hits > 0.5)
    total_hot = lax.psum(hot_grad, ("shard", "dp"))
    hot_out, hot_accum_out = adagrad_rows(hot_table, hot_accum, total_hot)
    return (cold_out, cold_accum_out, hot_out, hot_accum_out)


def solution(mesh):
    return jax.shard_map(
        on_device,
        mesh=mesh,
        in_specs=(
            P("shard", None),
            P("shard"),
            P("shard", None),
            P(),
            P(),
            P(),
            P(),
            P(),
            P(),
            P(("shard", "dp")),
            P(("shard", "dp"), None),
            P(("shard", "dp"), None),
            P(("shard", "dp"), None),
            P(("shard", "dp"), None),
        ),
        out_specs=(P("shard", None), P("shard"), P(), P()),
        check_vma=False,
    )
```

profile of v0, /device:TPU:8, one launch (start us, length us, event | category | flops | bytes accessed | tf_op | source)
XLA Modules:
  0.0 695.9 jit_solution(9611974366071185003)
XLA Ops:
  9.4 20.0 %all_to_all.62 = s32[32,1,64]{2,1,0:T(1,128)S(1)} all-to-all(s32[32,1,64]{2,1,0:T(1,128)S(1)} %bitcast.113), channel_id=1, replica_groups=mesh['shard'=32,'dp'=8] {'shard'}, dimensions={0} | all-to-all | bytes 16384 | tf_op jit(solution)/shard_map/all_to_all | solution.py:82
  29.4 4.9 all-to-all-start
  34.5 9.9 %gather_fusion.3 = bf16[2048,256]{1,0:T(8,128)(2,1)} fusion(bf16[2048,256]{1,0:T(8,128)(2,1)} %param.14, s32[2048]{0:T(1024)S(1)} %broadcast_clamp_fusion.3), kind=kCustom, calls=%fused_computation.3 | custom fusion | bytes 2105344 | tf_op jit(solution)/shard_map/gather | solution.py:84
  44.3 10.0 %all-to-all-start.6 = ((bf16[32,64,256]{2,1,0:T(8,128)(2,1)}), bf16[32,64,256]{2,1,0:T(8,128)(2,1)S(1)}, u32[]{:S(2)}, u32[]{:S(2)}) async-start(bf16[32,64,256]{2,1,0:T(8,128)(2,1)} %bitcast.16), calls=%async_computation.6 | async-start | bytes 2097152 | tf_op jit(solution)/shard_map/all_to_all | solution.py:83
  54.5 9.1 %gather_fusion = bf16[2048,256]{1,0:T(8,128)(2,1)} fusion(bf16[2048,256]{1,0:T(8,128)(2,1)S(1)} %copy-done.2, s32[2048]{0:T(1024)S(1)} %broadcast_clamp_fusion.5), kind=kCustom, calls=%fused_computation | custom fusion | bytes 2105344 | tf_op jit(solution)/shard_map/gather | solution.py:84
  63.5 17.2 %all-to-all-done.6 = bf16[32,64,256]{2,1,0:T(8,128)(2,1)S(1)} async-done(((bf16[32,64,256]{2,1,0:T(8,128)(2,1)}), bf16[32,64,256]{2,1,0:T(8,128)(2,1)S(1)}, u32[]{:S(2)}, u32[]{:S(2)}) %all-to-all-start.6) | async-done | bytes 1048608 | tf_op jit(solution)/shard_map/all_to_all | solution.py:83
  80.7 5.6 all-to-all-start.4
  98.1 8.4 %gather_fusion.5 = bf16[2048,256]{1,0:T(8,128)(2,1)} fusion(f32[1024,256]{1,0:T(8,128)S(1)} %copy-done.1, s32[2048]{0:T(1024)S(1)} %broadcast_clamp_fusion), kind=kCustom, calls=%fused_computation.5 | custom fusion | bytes 2105344 | tf_op jit(solution)/shard_map/gather | solution.py:90
  106.5 8.5 %gather_fusion.2 = bf16[2048,256]{1,0:T(8,128)(2,1)} fusion(f32[1024,256]{1,0:T(8,128)S(1)} %copy-done.1, s32[2048]{0:T(1024)S(1)} %broadcast_clamp_fusion.1), kind=kCustom, calls=%fused_computation.2 | custom fusion | bytes 2105344 | tf_op jit(solution)/shard_map/gather | solution.py:90
  115.0 9.0 %gather_fusion.4 = bf16[2048,256]{1,0:T(8,128)(2,1)} fusion(bf16[2048,256]{1,0:T(8,128)(2,1)S(1)} %bitcast.86, s32[2048]{0:T(1024)S(1)} %broadcast_clamp_fusion.2), kind=kCustom, calls=%fused_computation.4 | custom fusion | bytes 2105344 | tf_op jit(solution)/shard_map/gather | solution.py:89
  124.1 4.4 fusion.27
  129.9 10.5 %all-to-all-start.3 = ((s32[32,1,1]{2,1,0:T(1,128)}), s32[32,1,1]{2,1,0:T(1,128)}, u32[]{:S(2)}, u32[]{:S(2)}) async-start(s32[32,1,1]{2,1,0:T(1,128)} %copy.67), calls=%async_computation.3 | async-start | bytes 32768 | tf_op jit(solution)/shard_map/all_to_all | solution.py:110
  140.5 9.9 %gather_fusion.1 = bf16[2048,256]{1,0:T(8,128)(2,1)} fusion(bf16[2048,256]{1,0:T(8,128)(2,1)} %bitcast.6, s32[2048]{0:T(1024)S(1)} %broadcast_clamp_fusion.4), kind=kCustom, calls=%fused_computation.1 | custom fusion | bytes 2105344 | tf_op jit(solution)/shard_map/gather | solution.py:89
  150.3 4.3 fusion.28
  160.4 3.9 copy.84
  182.8 5.9 copy.83
  188.7 10.1 %all-to-all-start.1 = ((s32[32,1,1]{2,1,0:T(1,128)}), s32[32,1,1]{2,1,0:T(1,128)S(1)}, u32[]{:S(2)}, u32[]{:S(2)}) async-start(s32[32,1,1]{2,1,0:T(1,128)} %copy.66), calls=%async_computation.1 | async-start | bytes 32768 | tf_op jit(solution)/shard_map/all_to_all | solution.py:110
  198.8 5.8 bitcast_add_fusion.1
  204.6 13.5 %scatter_custom_fusion.2 = f32[2048,256]{1,0:T(8,128)} fusion(s32[2048]{0:T(1024)} %reshape.252, f32[256,16,256]{2,1,0:T(8,128)} %bitcast_add_fusion.1, f32[]{:T(128)} %constant.13.clone.1), kind=kCustom, calls=%fused_computation.25 | custom fusion | flops 524288 | bytes 4194816 | tf_op jit(solution)/shard_map/scatter-add | solution.py:94
  220.8 9.8 %all-to-all-start.5 = ((bf16[32,64,256]{2,1,0:T(8,128)(2,1)}), bf16[32,64,256]{2,1,0:T(8,128)(2,1)}, u32[]{:S(2)}, u32[]{:S(2)}) async-start(bf16[32,64,256]{2,1,0:T(8,128)(2,1)} %bitcast.104), calls=%async_computation.5 | async-start | bytes 2097152 | tf_op jit(solution)/shard_map/all_to_all | solution.py:107
  235.4 3.6 fusion.38
  243.7 13.6 %scatter_custom_fusion.4 = f32[2048,256]{1,0:T(8,128)} fusion(s32[2048]{0:T(1024)} %reshape.268, f32[256,16,256]{2,1,0:T(8,128)} %bitcast_add_fusion, f32[]{:T(128)} %constant.13.clone.1), kind=kCustom, calls=%fused_computation.23 | custom fusion | flops 524288 | bytes 4194816 | tf_op jit(solution)/shard_map/scatter-add | solution.py:94
  260.0 10.0 %all-to-all-start.7 = ((bf16[32,64,256]{2,1,0:T(8,128)(2,1)}), bf16[32,64,256]{2,1,0:T(8,128)(2,1)}, u32[]{:S(2)}, u32[]{:S(2)}) async-start(bf16[32,64,256]{2,1,0:T(8,128)(2,1)} %bitcast.24), calls=%async_computation.7 | async-start | bytes 2097152 | tf_op jit(solution)/shard_map/all_to_all | solution.py:107
  275.1 11.3 %scatter_custom_fusion.1 = f32[2048]{0:T(1024)S(1)} fusion(s32[2048]{0:T(1024)S(1)} %reshape.244, f32[2048]{0:T(1024)S(1)} %reshape.246, f32[]{:T(128)} %constant.13.clone.1), kind=kCustom, calls=%fused_computation.87 | custom fusion | flops 2048 | bytes 8196 | tf_op jit(solution)/shard_map/scatter-add | solution.py:118
  286.4 11.3 %scatter_custom_fusion = f32[2048]{0:T(1024)S(1)} fusion(s32[2048]{0:T(1024)S(1)} %reshape.236, f32[2048]{0:T(1024)S(1)} %reshape.238, f32[]{:T(128)} %constant.13.clone.1), kind=kCustom, calls=%fused_computation.89 | custom fusion | flops 2048 | bytes 8196 | tf_op jit(solution)/shard_map/scatter-add | solution.py:118
  297.7 12.4 %scatter_custom_fusion.6 = f32[1024,256]{1,0:T(8,128)S(1)} fusion(s32[2048]{0:T(1024)S(1)} %reshape.284, f32[256,16,256]{2,1,0:T(8,128)} %bitcast_add_fusion.1, f32[]{:T(128)} %constant.13.clone.1), kind=kCustom, calls=%fused_computation.21 | custom fusion | flops 524288 | bytes 3146240 | tf_op jit(solution)/shard_map/scatter-add | solution.py:99
  310.1 13.1 %scatter_custom_fusion.7 = f32[1024,256]{1,0:T(8,128)} fusion(s32[2048]{0:T(1024)S(1)} %reshape.292, f32[256,16,256]{2,1,0:T(8,128)} %bitcast_add_fusion, f32[]{:T(128)} %constant.13.clone.1), kind=kCustom, calls=%fused_computation.19 | custom fusion | flops 524288 | bytes 3146240 | tf_op jit(solution)/shard_map/scatter-add | solution.py:99
  325.6 12.4 %psum.21 = bf16[2048]{0:T(1024)(128)(2,1)S(1)} all-reduce(bf16[2048]{0:T(1024)(128)(2,1)S(1)} %add_convert_fusion.1), channel_id=1, replica_groups=mesh['shard'=32,'dp'=8] {'dp'}, use_global_device_ids=true, to_apply=%region_2.0 | all-reduce | flops 2048 | bytes 8192 | tf_op jit(solution)/shard_map/psum | solution.py:123
  338.1 247.5 %all-reduce.5.cloned.1.call-done = f32[1024,256]{1,0:T(8,128)} async-done(((f32[1024,256]{1,0:T(8,128)}), f32[1024,256]{1,0:T(8,128)}) %all-reduce.5.cloned.1.call-update) | async-done | bytes 1048592 | tf_op jit(solution)/shard_map/psum | solution.py:128
  587.0 12.6 %scatter_custom_fusion.3 = f32[2048,256]{1,0:T(8,128)} fusion(s32[2048]{0:T(1024)S(1)} %reshape.236, bf16[2048,256]{1,0:T(8,128)(2,1)} %bitcast.28, f32[]{:T(128)} %constant.13.clone.1), kind=kCustom, calls=%fused_computation.30 | custom fusion | flops 1048576 | bytes 3145732 | tf_op jit(solution)/shard_map/scatter-add | solution.py:112
  599.6 12.3 %scatter_custom_fusion.5 = f32[2048,256]{1,0:T(8,128)} fusion(s32[2048]{0:T(1024)S(1)} %reshape.244, bf16[2048,256]{1,0:T(8,128)(2,1)} %bitcast.29, f32[]{:T(128)} %constant.13.clone.1), kind=kCustom, calls=%fused_computation.28 | custom fusion | flops 1048576 | bytes 3145732 | tf_op jit(solution)/shard_map/scatter-add | solution.py:112
  617.3 64.7 %all-reduce.3.cloned.1.call-done = bf16[2048,256]{1,0:T(8,128)(2,1)} async-done(((bf16[2048,256]{1,0:T(8,128)(2,1)}), bf16[2048,256]{1,0:T(8,128)(2,1)}) %all-reduce.3.cloned.1.call-update) | async-done | bytes 1048592 | tf_op jit(solution)/shard_map/psum | solution.py:122
  (146 shorter events, 74.2 us)
Async XLA Ops:
  8.0 167.3 %copy-start = (bf16[256,512]{1,0:T(8,128)(2,1)S(1)}, bf16[256,512]{1,0:T(8,128)(2,1)}, u32[]{:S(2)}) copy-start(bf16[256,512]{1,0:T(8,128)(2,1)} %param.20) | copy-start | bytes 786436
  29.4 14.9 %copy-start.12 = (s32[32,1,64]{2,1,0:T(1,128)}, s32[32,1,64]{2,1,0:T(1,128)S(1)}, u32[]{:S(2)}) copy-start(s32[32,1,64]{2,1,0:T(1,128)S(1)} %all_to_all.62) | copy-start | bytes 24580
  29.4 14.9 %all-to-all-start = ((s32[32,1,64]{2,1,0:T(1,128)}), s32[32,1,64]{2,1,0:T(1,128)S(1)}, u32[]{:S(2)}, u32[]{:S(2)}) async-start(s32[32,1,64]{2,1,0:T(1,128)} %bitcast), calls=%async_computation | async-start | bytes 32768 | tf_op jit(solution)/shard_map/all_to_all | solution.py:82
  44.3 10.1 %copy-start.2 = (bf16[2048,256]{1,0:T(8,128)(2,1)S(1)}, bf16[2048,256]{1,0:T(8,128)(2,1)}, u32[]{:S(2)}) copy-start(bf16[2048,256]{1,0:T(8,128)(2,1)} %param.14) | copy-start | bytes 3145732
  44.3 36.4 %all-to-all-start.6 = ((bf16[32,64,256]{2,1,0:T(8,128)(2,1)}), bf16[32,64,256]{2,1,0:T(8,128)(2,1)S(1)}, u32[]{:S(2)}, u32[]{:S(2)}) async-start(bf16[32,64,256]{2,1,0:T(8,128)(2,1)} %bitcast.16), calls=%async_computation.6 | async-start | bytes 2097152 | tf_op jit(solution)/shard_map/all_to_all | solution.py:83
  63.5 22.8 %copy-start.27 = (s32[2,32]{1,0:T(2,128)S(1)}, s32[2,32]{1,0:T(2,128)}, u32[]{:S(2)}) copy-start(s32[2,32]{1,0:T(2,128)} %param.27) | copy-start | bytes 772
  63.5 24.2 %copy-start.21 = (s32[512,8]{0,1:T(8,128)S(1)}, s32[512,8]{0,1:T(8,128)}, u32[]{:S(2)}) copy-start(s32[512,8]{0,1:T(8,128)} %param.25) | copy-start | bytes 49156
  63.5 34.5 %copy-start.1 = (f32[1024,256]{1,0:T(8,128)S(1)}, f32[1024,256]{1,0:T(8,128)}, u32[]{:S(2)}) copy-start(f32[1024,256]{1,0:T(8,128)} %param.17) | copy-start | bytes 3145732
  80.7 49.2 %all-to-all-start.4 = ((bf16[32,64,256]{2,1,0:T(8,128)(2,1)}), bf16[32,64,256]{2,1,0:T(8,128)(2,1)}, u32[]{:S(2)}, u32[]{:S(2)}) async-start(bf16[32,64,256]{2,1,0:T(8,128)(2,1)} %bitcast.103), calls=%async_computation.4 | async-start | bytes 2097152 | tf_op jit(solution)/shard_map/all_to_all | solution.py:83
  98.1 8.4 %copy-start.18 = (s32[2048]{0:T(1024)S(1)}, s32[2048]{0:T(1024)}, u32[]{:S(2)}) copy-start(s32[2048]{0:T(1024)} %reshape.204) | copy-start | bytes 24580
  106.5 8.5 %copy-start.16 = (s32[2048]{0:T(1024)S(1)}, s32[2048]{0:T(1024)}, u32[]{:S(2)}) copy-start(s32[2048]{0:T(1024)} %reshape.196) | copy-start | bytes 24580
  106.5 8.5 %copy-start.17 = (s32[2048]{0:T(1024)S(1)}, s32[2048]{0:T(1024)}, u32[]{:S(2)}) copy-start(s32[2048]{0:T(1024)} %reshape.220) | copy-start | bytes 24580
  124.0 4.4 copy-start.4
  124.0 4.4 copy-start.5
  129.9 58.8 %all-to-all-start.3 = ((s32[32,1,1]{2,1,0:T(1,128)}), s32[32,1,1]{2,1,0:T(1,128)}, u32[]{:S(2)}, u32[]{:S(2)}) async-start(s32[32,1,1]{2,1,0:T(1,128)} %copy.67), calls=%async_computation.3 | async-start | bytes 32768 | tf_op jit(solution)/shard_map/all_to_all | solution.py:110
  150.3 4.3 copy-start.7
  150.3 4.3 copy-start.8
  168.4 2.8 copy-start.3
  188.7 32.0 %all-to-all-start.1 = ((s32[32,1,1]{2,1,0:T(1,128)}), s32[32,1,1]{2,1,0:T(1,128)S(1)}, u32[]{:S(2)}, u32[]{:S(2)}) async-start(s32[32,1,1]{2,1,0:T(1,128)} %copy.66), calls=%async_computation.1 | async-start | bytes 32768 | tf_op jit(solution)/shard_map/all_to_all | solution.py:110
  220.8 9.8 %copy-start.14 = (s32[32,1,1]{2,1,0:T(1,128)}, s32[32,1,1]{2,1,0:T(1,128)S(1)}, u32[]{:S(2)}) copy-start(s32[32,1,1]{2,1,0:T(1,128)S(1)} %all-to-all-done.1) | copy-start | bytes 388
  220.8 39.2 %all-to-all-start.5 = ((bf16[32,64,256]{2,1,0:T(8,128)(2,1)}), bf16[32,64,256]{2,1,0:T(8,128)(2,1)}, u32[]{:S(2)}, u32[]{:S(2)}) async-start(bf16[32,64,256]{2,1,0:T(8,128)(2,1)} %bitcast.104), calls=%async_computation.5 | async-start | bytes 2097152 | tf_op jit(solution)/shard_map/all_to_all | solution.py:107
  257.3 12.9 %copy-start.20 = (s32[256,8]{0,1:T(8,128)S(1)}, s32[256,8]{0,1:T(8,128)}, u32[]{:S(2)}) copy-start(s32[256,8]{0,1:T(8,128)} %get-tuple-element.14) | copy-start | bytes 24580
  257.3 13.2 %copy-start.19 = (s32[256,8]{0,1:T(8,128)S(1)}, s32[256,8]{0,1:T(8,128)}, u32[]{:S(2)}) copy-start(s32[256,8]{0,1:T(8,128)} %get-tuple-element.17) | copy-start | bytes 24580
  260.0 12.3 %copy-start.15 = (s32[32,1,1]{2,1,0:T(1,128)S(1)}, s32[32,1,1]{2,1,0:T(1,128)}, u32[]{:S(2)}) copy-start(s32[32,1,1]{2,1,0:T(1,128)} %copy-done.14) | copy-start | bytes 388
  260.0 13.6 %copy-start.13 = (s32[32,1,64]{2,1,0:T(1,128)S(1)}, s32[32,1,64]{2,1,0:T(1,128)}, u32[]{:S(2)}) copy-start(s32[32,1,64]{2,1,0:T(1,128)} %copy-done.12) | copy-start | bytes 24580
  260.0 339.7 %all-to-all-start.7 = ((bf16[32,64,256]{2,1,0:T(8,128)(2,1)}), bf16[32,64,256]{2,1,0:T(8,128)(2,1)}, u32[]{:S(2)}, u32[]{:S(2)}) async-start(bf16[32,64,256]{2,1,0:T(8,128)(2,1)} %bitcast.24), calls=%async_computation.7 | async-start | bytes 2097152 | tf_op jit(solution)/shard_map/all_to_all | solution.py:107
  269.9 315.6 %all-reduce.5.cloned.1.call-start = ((), (), s32[]{:S(2)}) async-start(), calls=%async_computation.9 | async-start | bytes 2097152 | tf_op jit(solution)/shard_map/psum | solution.py:128
  325.5 356.4 %all-reduce.3.cloned.1.call-start = ((), (), s32[]{:S(2)}) async-start(), calls=%async_computation.8 | async-start | bytes 2097152 | tf_op jit(solution)/shard_map/psum | solution.py:122
  611.9 3.5 copy-start.23
  611.9 4.1 copy-start.9
  616.1 67.8 %copy-start.22 = (f32[2048]{0:T(1024)S(1)}, f32[2048]{0:T(1024)}, u32[]{:S(2)}) copy-start(f32[2048]{0:T(1024)} %param.15) | copy-start | bytes 24580
  684.5 2.2 copy-start.11
  (5 other events, 7.1 us)
Sparse Core Ops, SparseCore 0:
  325.6 259.8 all-reduce.4
Sparse Core Ops, SparseCore 1:
  615.5 66.3 all-reduce.2
where the time goes:
time: 702 us; the launch traced here: 696 us
  waiting for transfers between devices  329 us (47%)
  other arithmetic  133 us (19%)
  local copies, waits for them, and re-layouts  92.7 us (13%)
  starting transfers between devices  61.3 us (9%)
  blocking collectives  32.5 us (5%)
  matrix products  30.5 us (4%)
  between operations  16.3 us (2%)
    psum x1, waiting for transfers between devices, on_device(): total_hot = lax.psum(hot_grad, ('shard', 'dp'))  248 us
    psum x1, waiting for transfers between devices, on_device(): lax.psum(cold_grad.astype(jnp.bfloat16), 'dp').astype(jnp.float32)  64.7 us
    scatter-add x2, other arithmetic, on_device(): jax.ops.segment_sum(gradients[:, :cold_feats].reshape(-1, row_width), slo...  27.1 us
    scatter-add x2, other arithmetic, on_device(): jax.ops.segment_sum(gradients[:, cold_feats:].reshape(-1, row_width), hot...  25.5 us
    scatter-add x2, other arithmetic, on_device(): jax.ops.segment_sum(owner_grad.reshape(-1, row_width), requested.reshape(...  24.9 us
    scatter-add x2, other arithmetic, on_device(): jax.ops.segment_sum(live_mask.reshape(-1), requested.reshape(-1), num_seg...  22.6 us
    all_to_all x2, starting transfers between devices, on_device(): lax.all_to_all(counts[micro_index], 'shard', split_axis=0, concat_axis=0,...  20.6 us
    all_to_all x1, blocking collectives, on_device(): lax.all_to_all(asked_rows, 'shard', split_axis=0, concat_axis=0, tiled=True)  20 us
  transfers between devices with their start and end apart: 9, of which 3 were waited for; matrix products, arithmetic and copies ran while one was open for 33% of the time, Pallas kernels for 0%

commit v1 on v0

--- a/solution.py
+++ b/solution.py
@@ -125,7 +125,9 @@
     averaged = summed_grad / jnp.maximum(summed_hits, 1.0)[:, None]
     updated, cold_accum_out = adagrad_rows(cold_table.astype(jnp.float32), cold_accum, averaged)
     cold_out = requantize(updated, dither_bits, summed_hits > 0.5)
-    total_hot = lax.psum(hot_grad, ("shard", "dp"))
+    total_hot = hot_grad
+    for mesh_axis in ("dp", "shard"):
+        total_hot = lax.psum(total_hot, mesh_axis)
     hot_out, hot_accum_out = adagrad_rows(hot_table, hot_accum, total_hot)
     return (cold_out, cold_accum_out, hot_out, hot_accum_out)
 

time: 702 us -> 634 us (0.903)
  waiting for transfers between devices: 329 us -> 262 us
    psum x1 -> x2, waiting for transfers between devices: 248 us -> 180 us  [on_device(): total_hot = lax.psum(total_hot, mesh_axis)]
  transfers between devices with their start and end apart: 9 -> 10, of which waited for: 3 -> 4; matrix products, arithmetic and copies ran while one was open for 33% -> 37% of each run, Pallas kernels for 0% -> 0%
where the time goes in v1:
time: 634 us; the launch traced here: 628 us
  waiting for transfers between devices  262 us (41%)
  other arithmetic  133 us (21%)
  local copies, waits for them, and re-layouts  92.7 us (15%)
  starting transfers between devices  61.2 us (10%)
  blocking collectives  33.7 us (5%)
  matrix products  30.5 us (5%)
  between operations  14.6 us (2%)
    psum x2, waiting for transfers between devices, on_device(): total_hot = lax.psum(total_hot, mesh_axis)  180 us
    psum x1, waiting for transfers between devices, on_device(): lax.psum(cold_grad.astype(jnp.bfloat16), 'dp').astype(jnp.float32)  64.7 us
    scatter-add x2, other arithmetic, on_device(): jax.ops.segment_sum(gradients[:, :cold_feats].reshape(-1, row_width), slo...  27.1 us
    scatter-add x2, other arithmetic, on_device(): jax.ops.segment_sum(gradients[:, cold_feats:].reshape(-1, row_width), hot...  25.5 us
    scatter-add x2, other arithmetic, on_device(): jax.ops.segment_sum(owner_grad.reshape(-1, row_width), requested.reshape(...  24.9 us
    scatter-add x2, other arithmetic, on_device(): jax.ops.segment_sum(live_mask.reshape(-1), requested.reshape(-1), num_seg...  22.6 us
    all_to_all x2, starting transfers between devices, on_device(): lax.all_to_all(counts[micro_index], 'shard', split_axis=0, concat_axis=0,...  20.6 us
    all_to_all x1, blocking collectives, on_device(): lax.all_to_all(asked_rows, 'shard', split_axis=0, concat_axis=0, tiled=True)  20 us
  transfers between devices with their start and end apart: 10, of which 4 were waited for; matrix products, arithmetic and copies ran while one was open for 37% of the time, Pallas kernels for 0%

profile of v1, /device:TPU:8, one launch (start us, length us, event | category | flops | bytes accessed | tf_op | source)
XLA Modules:
  0.0 627.8 jit_solution(10525574304037473116)
XLA Ops:
  8.6 20.0 %all_to_all.62 = s32[32,1,64]{2,1,0:T(1,128)S(1)} all-to-all(s32[32,1,64]{2,1,0:T(1,128)S(1)} %bitcast.113), channel_id=1, replica_groups=mesh['shard'=32,'dp'=8] {'shard'}, dimensions={0} | all-to-all | bytes 16384 | tf_op jit(solution)/shard_map/all_to_all | solution.py:82
  28.6 4.9 all-to-all-start
  33.6 9.9 %gather_fusion.3 = bf16[2048,256]{1,0:T(8,128)(2,1)} fusion(bf16[2048,256]{1,0:T(8,128)(2,1)} %param.14, s32[2048]{0:T(1024)S(1)} %broadcast_clamp_fusion.3), kind=kCustom, calls=%fused_computation.3 | custom fusion | bytes 2105344 | tf_op jit(solution)/shard_map/gather | solution.py:84
  43.5 10.0 %all-to-all-start.6 = ((bf16[32,64,256]{2,1,0:T(8,128)(2,1)}), bf16[32,64,256]{2,1,0:T(8,128)(2,1)S(1)}, u32[]{:S(2)}, u32[]{:S(2)}) async-start(bf16[32,64,256]{2,1,0:T(8,128)(2,1)} %bitcast.16), calls=%async_computation.6 | async-start | bytes 2097152 | tf_op jit(solution)/shard_map/all_to_all | solution.py:83
  53.6 9.1 %gather_fusion = bf16[2048,256]{1,0:T(8,128)(2,1)} fusion(bf16[2048,256]{1,0:T(8,128)(2,1)S(1)} %copy-done.2, s32[2048]{0:T(1024)S(1)} %broadcast_clamp_fusion.5), kind=kCustom, calls=%fused_computation | custom fusion | bytes 2105344 | tf_op jit(solution)/shard_map/gather | solution.py:84
  62.7 17.2 %all-to-all-done.6 = bf16[32,64,256]{2,1,0:T(8,128)(2,1)S(1)} async-done(((bf16[32,64,256]{2,1,0:T(8,128)(2,1)}), bf16[32,64,256]{2,1,0:T(8,128)(2,1)S(1)}, u32[]{:S(2)}, u32[]{:S(2)}) %all-to-all-start.6) | async-done | bytes 1048608 | tf_op jit(solution)/shard_map/all_to_all | solution.py:83
  79.9 5.6 all-to-all-start.4
  97.2 8.4 %gather_fusion.5 = bf16[2048,256]{1,0:T(8,128)(2,1)} fusion(f32[1024,256]{1,0:T(8,128)S(1)} %copy-done.1, s32[2048]{0:T(1024)S(1)} %broadcast_clamp_fusion), kind=kCustom, calls=%fused_computation.5 | custom fusion | bytes 2105344 | tf_op jit(solution)/shard_map/gather | solution.py:90
  105.7 8.5 %gather_fusion.2 = bf16[2048,256]{1,0:T(8,128)(2,1)} fusion(f32[1024,256]{1,0:T(8,128)S(1)} %copy-done.1, s32[2048]{0:T(1024)S(1)} %broadcast_clamp_fusion.1), kind=kCustom, calls=%fused_computation.2 | custom fusion | bytes 2105344 | tf_op jit(solution)/shard_map/gather | solution.py:90
  114.2 9.0 %gather_fusion.4 = bf16[2048,256]{1,0:T(8,128)(2,1)} fusion(bf16[2048,256]{1,0:T(8,128)(2,1)S(1)} %bitcast.86, s32[2048]{0:T(1024)S(1)} %broadcast_clamp_fusion.2), kind=kCustom, calls=%fused_computation.4 | custom fusion | bytes 2105344 | tf_op jit(solution)/shard_map/gather | solution.py:89
  123.2 4.4 fusion.27
  129.1 10.5 %all-to-all-start.3 = ((s32[32,1,1]{2,1,0:T(1,128)}), s32[32,1,1]{2,1,0:T(1,128)}, u32[]{:S(2)}, u32[]{:S(2)}) async-start(s32[32,1,1]{2,1,0:T(1,128)} %copy.67), calls=%async_computation.3 | async-start | bytes 32768 | tf_op jit(solution)/shard_map/all_to_all | solution.py:110
  139.6 9.9 %gather_fusion.1 = bf16[2048,256]{1,0:T(8,128)(2,1)} fusion(bf16[2048,256]{1,0:T(8,128)(2,1)} %bitcast.6, s32[2048]{0:T(1024)S(1)} %broadcast_clamp_fusion.4), kind=kCustom, calls=%fused_computation.1 | custom fusion | bytes 2105344 | tf_op jit(solution)/shard_map/gather | solution.py:89
  149.5 4.3 fusion.28
  159.5 3.9 copy.84
  182.0 5.9 copy.83
  187.9 10.1 %all-to-all-start.1 = ((s32[32,1,1]{2,1,0:T(1,128)}), s32[32,1,1]{2,1,0:T(1,128)S(1)}, u32[]{:S(2)}, u32[]{:S(2)}) async-start(s32[32,1,1]{2,1,0:T(1,128)} %copy.66), calls=%async_computation.1 | async-start | bytes 32768 | tf_op jit(solution)/shard_map/all_to_all | solution.py:110
  198.0 5.8 bitcast_add_fusion.1
  203.7 13.5 %scatter_custom_fusion.2 = f32[2048,256]{1,0:T(8,128)} fusion(s32[2048]{0:T(1024)} %reshape.252, f32[256,16,256]{2,1,0:T(8,128)} %bitcast_add_fusion.1, f32[]{:T(128)} %constant.13.clone.1), kind=kCustom, calls=%fused_computation.25 | custom fusion | flops 524288 | bytes 4194816 | tf_op jit(solution)/shard_map/scatter-add | solution.py:94
  219.9 9.8 %all-to-all-start.5 = ((bf16[32,64,256]{2,1,0:T(8,128)(2,1)}), bf16[32,64,256]{2,1,0:T(8,128)(2,1)}, u32[]{:S(2)}, u32[]{:S(2)}) async-start(bf16[32,64,256]{2,1,0:T(8,128)(2,1)} %bitcast.104), calls=%async_computation.5 | async-start | bytes 2097152 | tf_op jit(solution)/shard_map/all_to_all | solution.py:107
  242.8 13.6 %scatter_custom_fusion.4 = f32[2048,256]{1,0:T(8,128)} fusion(s32[2048]{0:T(1024)} %reshape.268, f32[256,16,256]{2,1,0:T(8,128)} %bitcast_add_fusion, f32[]{:T(128)} %constant.13.clone.1), kind=kCustom, calls=%fused_computation.23 | custom fusion | flops 524288 | bytes 4194816 | tf_op jit(solution)/shard_map/scatter-add | solution.py:94
  259.1 9.8 %all-to-all-start.7 = ((bf16[32,64,256]{2,1,0:T(8,128)(2,1)}), bf16[32,64,256]{2,1,0:T(8,128)(2,1)}, u32[]{:S(2)}, u32[]{:S(2)}) async-start(bf16[32,64,256]{2,1,0:T(8,128)(2,1)} %bitcast.24), calls=%async_computation.7 | async-start | bytes 2097152 | tf_op jit(solution)/shard_map/all_to_all | solution.py:107
  269.7 12.4 %scatter_custom_fusion.6 = f32[1024,256]{1,0:T(8,128)S(1)} fusion(s32[2048]{0:T(1024)S(1)} %reshape.284, f32[256,16,256]{2,1,0:T(8,128)} %bitcast_add_fusion.1, f32[]{:T(128)} %constant.13.clone.1), kind=kCustom, calls=%fused_computation.21 | custom fusion | flops 524288 | bytes 3146240 | tf_op jit(solution)/shard_map/scatter-add | solution.py:99
  282.1 13.1 %scatter_custom_fusion.7 = f32[1024,256]{1,0:T(8,128)} fusion(s32[2048]{0:T(1024)S(1)} %reshape.292, f32[256,16,256]{2,1,0:T(8,128)} %bitcast_add_fusion, f32[]{:T(128)} %constant.13.clone.1), kind=kCustom, calls=%fused_computation.19 | custom fusion | flops 524288 | bytes 3146240 | tf_op jit(solution)/shard_map/scatter-add | solution.py:99
  299.0 67.3 %all-reduce.6.cloned.1.call-done = f32[1024,256]{1,0:T(8,128)} async-done(((f32[1024,256]{1,0:T(8,128)}), f32[1024,256]{1,0:T(8,128)}) %all-reduce.6.cloned.1.call-update) | async-done | bytes 1048592 | tf_op jit(solution)/shard_map/psum | solution.py:130
  369.4 11.3 %scatter_custom_fusion.1 = f32[2048]{0:T(1024)S(1)} fusion(s32[2048]{0:T(1024)S(1)} %reshape.244, f32[2048]{0:T(1024)S(1)} %reshape.246, f32[]{:T(128)} %constant.13.clone.1), kind=kCustom, calls=%fused_computation.87 | custom fusion | flops 2048 | bytes 8196 | tf_op jit(solution)/shard_map/scatter-add | solution.py:118
  380.7 11.3 %scatter_custom_fusion = f32[2048]{0:T(1024)S(1)} fusion(s32[2048]{0:T(1024)S(1)} %reshape.236, f32[2048]{0:T(1024)S(1)} %reshape.238, f32[]{:T(128)} %constant.13.clone.1), kind=kCustom, calls=%fused_computation.89 | custom fusion | flops 2048 | bytes 8196 | tf_op jit(solution)/shard_map/scatter-add | solution.py:118
  392.0 13.7 %psum.28 = bf16[2048]{0:T(1024)(128)(2,1)S(1)} all-reduce(bf16[2048]{0:T(1024)(128)(2,1)S(1)} %add_convert_fusion.1), channel_id=1, replica_groups=mesh['shard'=32,'dp'=8] {'dp'}, use_global_device_ids=true, to_apply=%region_2.0 | all-reduce | flops 2048 | bytes 8192 | tf_op jit(solution)/shard_map/psum | solution.py:123
  405.7 112.6 %all-reduce.8.cloned.1.call-done = f32[1024,256]{1,0:T(8,128)} async-done(((f32[1024,256]{1,0:T(8,128)}), f32[1024,256]{1,0:T(8,128)}) %all-reduce.8.cloned.1.call-update) | async-done | bytes 1048592 | tf_op jit(solution)/shard_map/psum | solution.py:130
  519.8 12.6 %scatter_custom_fusion.3 = f32[2048,256]{1,0:T(8,128)} fusion(s32[2048]{0:T(1024)S(1)} %reshape.236, bf16[2048,256]{1,0:T(8,128)(2,1)} %bitcast.28, f32[]{:T(128)} %constant.13.clone.1), kind=kCustom, calls=%fused_computation.30 | custom fusion | flops 1048576 | bytes 3145732 | tf_op jit(solution)/shard_map/scatter-add | solution.py:112
  532.4 12.3 %scatter_custom_fusion.5 = f32[2048,256]{1,0:T(8,128)} fusion(s32[2048]{0:T(1024)S(1)} %reshape.244, bf16[2048,256]{1,0:T(8,128)(2,1)} %bitcast.29, f32[]{:T(128)} %constant.13.clone.1), kind=kCustom, calls=%fused_computation.28 | custom fusion | flops 1048576 | bytes 3145732 | tf_op jit(solution)/shard_map/scatter-add | solution.py:112
  550.0 64.7 %all-reduce.4.cloned.1.call-done = bf16[2048,256]{1,0:T(8,128)(2,1)} async-done(((bf16[2048,256]{1,0:T(8,128)(2,1)}), bf16[2048,256]{1,0:T(8,128)(2,1)}) %all-reduce.4.cloned.1.call-update) | async-done | bytes 1048592 | tf_op jit(solution)/shard_map/psum | solution.py:122
  (149 shorter events, 77.8 us)
Async XLA Ops:
  7.2 167.3 %copy-start = (bf16[256,512]{1,0:T(8,128)(2,1)S(1)}, bf16[256,512]{1,0:T(8,128)(2,1)}, u32[]{:S(2)}) copy-start(bf16[256,512]{1,0:T(8,128)(2,1)} %param.20) | copy-start | bytes 786436
  28.6 14.9 %copy-start.12 = (s32[32,1,64]{2,1,0:T(1,128)}, s32[32,1,64]{2,1,0:T(1,128)S(1)}, u32[]{:S(2)}) copy-start(s32[32,1,64]{2,1,0:T(1,128)S(1)} %all_to_all.62) | copy-start | bytes 24580
  28.6 14.9 %all-to-all-start = ((s32[32,1,64]{2,1,0:T(1,128)}), s32[32,1,64]{2,1,0:T(1,128)S(1)}, u32[]{:S(2)}, u32[]{:S(2)}) async-start(s32[32,1,64]{2,1,0:T(1,128)} %bitcast), calls=%async_computation | async-start | bytes 32768 | tf_op jit(solution)/shard_map/all_to_all | solution.py:82
  43.5 10.1 %copy-start.2 = (bf16[2048,256]{1,0:T(8,128)(2,1)S(1)}, bf16[2048,256]{1,0:T(8,128)(2,1)}, u32[]{:S(2)}) copy-start(bf16[2048,256]{1,0:T(8,128)(2,1)} %param.14) | copy-start | bytes 3145732
  43.5 36.4 %all-to-all-start.6 = ((bf16[32,64,256]{2,1,0:T(8,128)(2,1)}), bf16[32,64,256]{2,1,0:T(8,128)(2,1)S(1)}, u32[]{:S(2)}, u32[]{:S(2)}) async-start(bf16[32,64,256]{2,1,0:T(8,128)(2,1)} %bitcast.16), calls=%async_computation.6 | async-start | bytes 2097152 | tf_op jit(solution)/shard_map/all_to_all | solution.py:83
  62.7 22.8 %copy-start.27 = (s32[2,32]{1,0:T(2,128)S(1)}, s32[2,32]{1,0:T(2,128)}, u32[]{:S(2)}) copy-start(s32[2,32]{1,0:T(2,128)} %param.27) | copy-start | bytes 772
  62.7 24.2 %copy-start.21 = (s32[512,8]{0,1:T(8,128)S(1)}, s32[512,8]{0,1:T(8,128)}, u32[]{:S(2)}) copy-start(s32[512,8]{0,1:T(8,128)} %param.25) | copy-start | bytes 49156
  62.7 34.5 %copy-start.1 = (f32[1024,256]{1,0:T(8,128)S(1)}, f32[1024,256]{1,0:T(8,128)}, u32[]{:S(2)}) copy-start(f32[1024,256]{1,0:T(8,128)} %param.17) | copy-start | bytes 3145732
  79.9 49.2 %all-to-all-start.4 = ((bf16[32,64,256]{2,1,0:T(8,128)(2,1)}), bf16[32,64,256]{2,1,0:T(8,128)(2,1)}, u32[]{:S(2)}, u32[]{:S(2)}) async-start(bf16[32,64,256]{2,1,0:T(8,128)(2,1)} %bitcast.103), calls=%async_computation.4 | async-start | bytes 2097152 | tf_op jit(solution)/shard_map/all_to_all | solution.py:83
  97.2 8.4 %copy-start.18 = (s32[2048]{0:T(1024)S(1)}, s32[2048]{0:T(1024)}, u32[]{:S(2)}) copy-start(s32[2048]{0:T(1024)} %reshape.204) | copy-start | bytes 24580
  105.7 8.5 %copy-start.16 = (s32[2048]{0:T(1024)S(1)}, s32[2048]{0:T(1024)}, u32[]{:S(2)}) copy-start(s32[2048]{0:T(1024)} %reshape.196) | copy-start | bytes 24580
  105.7 8.5 %copy-start.17 = (s32[2048]{0:T(1024)S(1)}, s32[2048]{0:T(1024)}, u32[]{:S(2)}) copy-start(s32[2048]{0:T(1024)} %reshape.220) | copy-start | bytes 24580
  123.2 4.4 copy-start.4
  123.2 4.4 copy-start.5
  129.1 58.8 %all-to-all-start.3 = ((s32[32,1,1]{2,1,0:T(1,128)}), s32[32,1,1]{2,1,0:T(1,128)}, u32[]{:S(2)}, u32[]{:S(2)}) async-start(s32[32,1,1]{2,1,0:T(1,128)} %copy.67), calls=%async_computation.3 | async-start | bytes 32768 | tf_op jit(solution)/shard_map/all_to_all | solution.py:110
  149.5 4.3 copy-start.7
  149.5 4.3 copy-start.8
  167.6 2.8 copy-start.3
  187.9 32.0 %all-to-all-start.1 = ((s32[32,1,1]{2,1,0:T(1,128)}), s32[32,1,1]{2,1,0:T(1,128)S(1)}, u32[]{:S(2)}, u32[]{:S(2)}) async-start(s32[32,1,1]{2,1,0:T(1,128)} %copy.66), calls=%async_computation.1 | async-start | bytes 32768 | tf_op jit(solution)/shard_map/all_to_all | solution.py:110
  219.9 9.8 %copy-start.14 = (s32[32,1,1]{2,1,0:T(1,128)}, s32[32,1,1]{2,1,0:T(1,128)S(1)}, u32[]{:S(2)}) copy-start(s32[32,1,1]{2,1,0:T(1,128)S(1)} %all-to-all-done.1) | copy-start | bytes 388
  219.9 39.2 %all-to-all-start.5 = ((bf16[32,64,256]{2,1,0:T(8,128)(2,1)}), bf16[32,64,256]{2,1,0:T(8,128)(2,1)}, u32[]{:S(2)}, u32[]{:S(2)}) async-start(bf16[32,64,256]{2,1,0:T(8,128)(2,1)} %bitcast.104), calls=%async_computation.5 | async-start | bytes 2097152 | tf_op jit(solution)/shard_map/all_to_all | solution.py:107
  256.4 12.8 %copy-start.20 = (s32[256,8]{0,1:T(8,128)S(1)}, s32[256,8]{0,1:T(8,128)}, u32[]{:S(2)}) copy-start(s32[256,8]{0,1:T(8,128)} %get-tuple-element.14) | copy-start | bytes 24580
  256.4 13.1 %copy-start.19 = (s32[256,8]{0,1:T(8,128)S(1)}, s32[256,8]{0,1:T(8,128)}, u32[]{:S(2)}) copy-start(s32[256,8]{0,1:T(8,128)} %get-tuple-element.17) | copy-start | bytes 24580
  259.1 273.3 %all-to-all-start.7 = ((bf16[32,64,256]{2,1,0:T(8,128)(2,1)}), bf16[32,64,256]{2,1,0:T(8,128)(2,1)}, u32[]{:S(2)}, u32[]{:S(2)}) async-start(bf16[32,64,256]{2,1,0:T(8,128)(2,1)} %bitcast.24), calls=%async_computation.7 | async-start | bytes 2097152 | tf_op jit(solution)/shard_map/all_to_all | solution.py:107
  269.0 97.4 %all-reduce.6.cloned.1.call-start = ((), (), s32[]{:S(2)}) async-start(), calls=%async_computation.9 | async-start | bytes 2097152 | tf_op jit(solution)/shard_map/psum | solution.py:130
  295.2 71.4 %copy-start.15 = (s32[32,1,1]{2,1,0:T(1,128)S(1)}, s32[32,1,1]{2,1,0:T(1,128)}, u32[]{:S(2)}) copy-start(s32[32,1,1]{2,1,0:T(1,128)} %copy-done.14) | copy-start | bytes 388
  295.2 72.7 %copy-start.13 = (s32[32,1,64]{2,1,0:T(1,128)S(1)}, s32[32,1,64]{2,1,0:T(1,128)}, u32[]{:S(2)}) copy-start(s32[32,1,64]{2,1,0:T(1,128)} %copy-done.12) | copy-start | bytes 24580
  297.6 220.8 %all-reduce.8.cloned.1.call-start = ((), (), s32[]{:S(2)}) async-start(), calls=%async_computation.10 | async-start | bytes 2097152 | tf_op jit(solution)/shard_map/psum | solution.py:130
  366.4 248.4 %all-reduce.4.cloned.1.call-start = ((), (), s32[]{:S(2)}) async-start(), calls=%async_computation.8 | async-start | bytes 2097152 | tf_op jit(solution)/shard_map/psum | solution.py:122
  544.7 3.5 copy-start.23
  544.7 4.1 copy-start.9
  548.9 67.8 %copy-start.22 = (f32[2048]{0:T(1024)S(1)}, f32[2048]{0:T(1024)}, u32[]{:S(2)}) copy-start(f32[2048]{0:T(1024)} %param.15) | copy-start | bytes 24580
  (6 other events, 9.3 us)
Sparse Core Ops, SparseCore 0:
  297.7 68.5 all-reduce.5
  369.8 148.5 all-reduce.7
  548.4 66.3 all-reduce.3
